TPU v7x, 128 devices: a whole 4x4x4 slice. The times are simulated.
128 devices in a mesh: section: 2 (over core), seq: 16 (over z, y), head: 4 (over x).
Axes of the slice: x: 4, y: 4, z: 4, core: 2. Of those that a mesh axis runs over, the one named last changes fastest.
Arguments:
- query_vectors: bfloat16 [2, 2048, 8192], P('section', 'seq', 'head'), may hold values from -400 to 400
- key_vectors: bfloat16 [2, 2048, 8192], P('section', 'seq', 'head'), may hold values from -6 to 6
- value_vectors: bfloat16 [2, 2048, 8192], P('section', 'seq', 'head'), may hold values from -6 to 6
- prior_state: float32 [2, 64, 128, 128], P('section', 'head'), may hold values from -128 to 128
- doc_ids: int32 [2, 2048], P('section', 'seq'), may hold values from 0 to 3, never falling along the last dimension, each value on 1 to 1024 neighbouring positions
- norm_gain: float32 [2, 8192], P('section', 'head'), may hold values from 0.25 to 1.75
- residual: bfloat16 [2, 2048, 6144], P('section', 'head', 'seq'), may hold values from -6 to 6
- out_weight: bfloat16 [2, 8192, 6144], P('section', 'head', 'seq'), may hold values from -0.0625 to 0.0625
- enc_weight: bfloat16 [2, 6144, 32768], P('section', None, ('seq', 'head')), may hold values from -0.078125 to 0.078125
- enc_bias: float32 [2, 32768], P('section', ('seq', 'head')), may hold values from -5 to 5
Outputs:
- handoff: bfloat16 [2, 2048, 6144], P('section', 'head', 'seq')
- monitor: bfloat16 [2, 32, 32768], P('section', None, ('seq', 'head'))
Inputs may be any that keep to these rules, and one draw needn't show every extreme that they name: `doc_ids`: document numbers never fall along a section's tokens, are 0 at its first token and rise by at most 1 from one token to the next; a document has at most 1024 tokens, and one has exactly that many.
All inputs are finite; a program needn't handle non-finite values.
Results may differ from a plain program's by a relative error of at most 0.0039.
Values may be sent and summed in bfloat16 or wider, within the bound.
No kernel may reach another device: no remote copies, remote signals or barrier semaphores. Data moves between devices by JAX's collectives and lax.ppermute only.
A program may use at most 128 MiB of HBM per device.

v0:
```python
import jax
import jax.numpy as jnp
from jax import lax
from jax.sharding import PartitionSpec as P

HD = 128
POOL = 64
HDIM = 8192
epsilon = 1e-06


def entering(part, axis, combine, identity):
    place = lax.axis_index(axis)
    gathered = jax.tree.map(lambda a: lax.all_gather(a, axis), part)
    state = jax.tree.map(lambda a, e: jnp.zeros_like(a) + jnp.asarray(e, a.dtype), part, identity)

    def one(hop, state):
        return combine(
            state, jax.tree.map(lambda a: lax.dynamic_index_in_dim(a, hop, 0, False), gathered)
        )

    return lax.fori_loop(0, place, one, state)


def passed_along(x, axis, by):
    devices = lax.axis_size(axis)
    return lax.ppermute(x, axis, [(i, (i + by) % devices) for i in range(devices)])


def merge_states(first_pair, second_pair):
    first_state, first_doc = first_pair
    second_state, second_doc = second_pair
    top_doc = jnp.maximum(first_doc, second_doc)
    merged = jnp.where(first_doc == top_doc, first_state, 0.0) + jnp.where(
        second_doc == top_doc, second_state, 0.0
    )
    return (merged, top_doc)


def local(
    query_vectors,
    key_vectors,
    value_vectors,
    prior_state,
    doc_ids,
    norm_gain,
    residual,
    out_weight,
    enc_weight,
    enc_bias,
):
    highest = lax.Precision.HIGHEST
    row_count = query_vectors.shape[1]
    local_heads = query_vectors.shape[2] // HD
    queries = query_vectors[0].reshape(row_count, local_heads, HD)
    keys_block = key_vectors[0].reshape(row_count, local_heads, HD)
    values_block = value_vectors[0].reshape(row_count, local_heads, HD)
    doc_index = doc_ids[0]
    doc_float = doc_index.astype(jnp.float32)
    last_doc = doc_float[-1]
    keys_last = jnp.where(
        (doc_index == doc_index[-1])[:, None, None], keys_block, jnp.zeros_like(keys_block)
    )
    summary = jnp.einsum(
        "thd,the->hde", keys_last, values_block, preferred_element_type=jnp.float32
    )
    identity_pair = (jnp.zeros_like(summary), jnp.full((1,), -1.0, jnp.float32))
    earlier_state, earlier_last = entering(
        (summary, last_doc[None]), "seq", merge_states, identity_pair
    )
    earlier_doc = earlier_last[0]
    incoming_state, incoming_doc = merge_states(
        (prior_state[0], jnp.zeros((), jnp.float32)), (earlier_state, earlier_doc)
    )
    inter = jnp.einsum(
        "thd,hde->the", queries.astype(jnp.float32), incoming_state, precision=highest
    )
    inter = inter * (doc_float == incoming_doc).astype(jnp.float32)[:, None, None]
    scores = jnp.einsum("thd,uhd->htu", queries, keys_block, preferred_element_type=jnp.float32)
    positions = jnp.arange(row_count)
    same_doc = (positions[None, :] <= positions[:, None]) & (
        doc_index[:, None] == doc_index[None, :]
    )
    scores = jnp.where(same_doc[None, :, :], scores, 0.0)
    intra = jnp.einsum("htu,uhe->the", scores, values_block.astype(jnp.float32), precision=highest)
    attended = (inter + intra).reshape(row_count, local_heads * HD)
    total_square = lax.psum(jnp.sum(attended * attended, axis=1), "head")
    inverse_rms = lax.rsqrt(total_square / HDIM + epsilon)
    normed = (attended * inverse_rms[:, None] * norm_gain[0]).astype(jnp.bfloat16)
    projection = out_weight[0]
    partial_sums = jnp.dot(
        lax.all_gather(normed, "seq", axis=0, tiled=True),
        projection,
        preferred_element_type=jnp.float32,
    )
    own_rows = residual[0]
    encoder = enc_weight[0]
    latent_width = encoder.shape[1]
    reduced = lax.psum_scatter(partial_sums, "head", scatter_dimension=0, tiled=True)
    layer_out = (own_rows.astype(jnp.float32) + reduced).astype(jnp.bfloat16)
    features = lax.all_gather(layer_out, "head", axis=0, tiled=True)
    pre_scores = jnp.dot(
        lax.all_gather(features, "seq", axis=1, tiled=True),
        encoder,
        preferred_element_type=jnp.float32,
    )
    latent = jax.nn.relu(pre_scores + enc_bias[0])
    pooled = jnp.mean(latent.reshape(-1, POOL, latent_width), axis=1).astype(jnp.bfloat16)
    handoff, monitor = passed_along((layer_out[None], pooled[None]), "section", 1)
    return (handoff, monitor)


def solution(mesh):
    return jax.shard_map(
        local,
        mesh=mesh,
        in_specs=(
            P("section", "seq", "head"),
            P("section", "seq", "head"),
            P("section", "seq", "head"),
            P("section", "head", None, None),
            P("section", "seq"),
            P("section", "head"),
            P("section", "head", "seq"),
            P("section", "head", "seq"),
            P("section", None, ("seq", "head")),
            P("section", ("seq", "head")),
        ),
        out_specs=(P("section", "head", "seq"), P("section", None, ("seq", "head"))),
        check_vma=False,
    )
```

profile of v0, /device:TPU:1, one launch (start us, length us, event | category | flops | bytes accessed | tf_op | source)
XLA Modules:
  0.0 542.9 jit_solution(13562496052584884869)
XLA Ops:
  7.2 1.3 slice.8
  8.6 1.3 broadcast_compare_fusion
  9.9 1.3 copy.23
  11.2 1.3 copy.24
  12.5 1.5 fusion.14
  14.1 1.2 dynamic-slice
  16.0 0.8 slice_dynamic-update-slice_fusion
  16.8 35.9 %all-reduce = f32[16]{0:T(128)S(1)} all-reduce(f32[16]{0:T(128)S(1)} %slice_dynamic-update-slice_fusion), channel_id=2, replica_groups=mesh['section'=2,'seq'=16,'head'=4] {'seq'}, use_global_device_ids=true, to_apply=%add | all-reduce | flops 16 | bytes 128
  52.8 1.1 copy.25
  54.3 2.2 convolution_bitcast_fusion
  56.5 72.5 %all-gather.13.cloned.1.call-done = f32[256,128,128]{2,1,0:T(8,128)} async-done(((f32[16,128,128]{2,1,0:T(8,128)}), f32[256,128,128]{2,1,0:T(8,128)}) %all-gather.13.cloned.1.call-update) | async-done | bytes 16777232 | tf_op jit(solution)/shard_map/all_gather | solution.py:14
  129.1 3.6 multiply_reduce_fusion
  132.7 8.4 %psum.7 = f32[128]{0:T(128)S(1)} all-reduce(f32[128]{0:T(128)S(1)} %get-tuple-element.50), channel_id=1, replica_groups=mesh['section'=2,'seq'=16,'head'=4] {'head'}, use_global_device_ids=true, to_apply=%region_3.4 | all-reduce | flops 128 | bytes 1024 | tf_op jit(solution)/shard_map/psum | solution.py:87
  141.1 2.4 fusion.9
  143.6 128.4 %all-gather.7.cloned.1.call-done = bf16[2048,2048]{0,1:T(8,128)(2,1)} async-done(((bf16[128,2048]{0,1:T(8,128)(2,1)}), bf16[2048,2048]{0,1:T(8,128)(2,1)}) %all-gather.7.cloned.1.call-update) | async-done | bytes 8388624 | tf_op jit(solution)/shard_map/all_gather | solution.py:92
  272.0 8.7 %fusion.4 = f32[2048,384]{1,0:T(8,128)} fusion(bf16[2048,2048]{0,1:T(8,128)(2,1)} %all-gather.7.cloned.1.call-done, bf16[1,2048,384]{2,1,0:T(8,128)(2,1)S(1)} %copy-done), kind=kOutput, calls=%fused_computation.6 | convolution fusion | flops 3221225472 | bytes 13107200 | tf_op jit(solution)/shard_map/dot_general | solution.py:91
  280.7 38.5 %reduce-scatter.2.cloned.1.call-done = f32[512,384]{1,0:T(8,128)} async-done(((f32[2048,384]{1,0:T(8,128)}), f32[512,384]{1,0:T(8,128)}) %reduce-scatter.2.cloned.1.call-update) | async-done | bytes 786448 | tf_op jit(solution)/shard_map/reduce_scatter | solution.py:99
  319.2 1.9 fusion.12
  321.2 26.3 %all-gather.9.cloned.1.call-done = bf16[2048,384]{1,0:T(8,128)(2,1)} async-done(((bf16[512,384]{1,0:T(8,128)(2,1)}), bf16[2048,384]{1,0:T(8,128)(2,1)}) %all-gather.9.cloned.1.call-update) | async-done | bytes 1572880 | tf_op jit(solution)/shard_map/all_gather | solution.py:101
  347.6 0.8 collective-permute-start
  348.3 164.4 %all-gather.11.cloned.1.call-done = bf16[2048,6144]{1,0:T(8,128)(2,1)} async-done(((bf16[2048,384]{1,0:T(8,128)(2,1)}), bf16[2048,6144]{1,0:T(8,128)(2,1)}) %all-gather.11.cloned.1.call-update) | async-done | bytes 25165840 | tf_op jit(solution)/shard_map/all_gather | solution.py:103
  512.7 19.8 %bitcast_reduce_fusion = f32[32,512]{1,0:T(8,128)S(1)} fusion(bf16[2048,6144]{1,0:T(8,128)(2,1)} %all-gather.11.cloned.1.call-done, bf16[1,6144,512]{2,1,0:T(8,128)(2,1)} %param.20, f32[512]{0:T(512)S(1)} %bitcast.80), kind=kOutput, calls=%fused_computation.4 | convolution fusion | flops 12888031232 | bytes 31524864 | tf_op jit(solution)/shard_map/dot_general | solution.py:102
  532.5 1.6 collective-permute-start.1
  534.1 0.9 collective-permute-done.1
  (34 shorter events, 2.8 us)
Async XLA Ops:
  7.2 264.8 %copy-start = (bf16[1,2048,384]{2,1,0:T(8,128)(2,1)S(1)}, bf16[1,2048,384]{2,1,0:T(8,128)(2,1)}, u32[]{:S(2)}) copy-start(bf16[1,2048,384]{2,1,0:T(8,128)(2,1)} %param.19) | copy-start | bytes 4718596
  7.2 46.7 %copy-start.4 = (s32[1,128]{1,0:T(1,128)S(1)}, s32[1,128]{1,0:T(1,128)}, u32[]{:S(2)}) copy-start(s32[1,128]{1,0:T(1,128)} %param.16) | copy-start | bytes 1540
  7.2 121.8 %all-gather.13.cloned.1.call-start = ((), (), s32[]{:S(2)}) async-start(), calls=%async_computation.5 | async-start | bytes 17825792 | tf_op jit(solution)/shard_map/all_gather | solution.py:14
  14.1 257.9 %all-gather.7.cloned.1.call-start = ((), (), s32[]{:S(2)}) async-start(), calls=%async_computation.1 | async-start | bytes 8912896 | tf_op jit(solution)/shard_map/all_gather | solution.py:92
  129.1 12.0 %copy-start.3 = (f32[1,2048]{1,0:T(1,128)S(1)}, f32[1,2048]{1,0:T(1,128)}, u32[]{:S(2)}) copy-start(f32[1,2048]{1,0:T(1,128)} %param.17) | copy-start | bytes 24580
  143.5 175.7 %copy-start.2 = (bf16[1,512,384]{2,1,0:T(8,128)(2,1)S(1)}, bf16[1,512,384]{2,1,0:T(8,128)(2,1)}, u32[]{:S(2)}) copy-start(bf16[1,512,384]{2,1,0:T(8,128)(2,1)} %param.18) | copy-start | bytes 1179652
  143.5 175.6 %reduce-scatter.2.cloned.1.call-start = ((), (), s32[]{:S(2)}) async-start(), calls=%async_computation.2 | async-start | bytes 3932160 | tf_op jit(solution)/shard_map/reduce_scatter | solution.py:99
  280.7 232.0 %copy-start.5 = (f32[1,512]{1,0:T(1,128)S(1)}, f32[1,512]{1,0:T(1,128)}, u32[]{:S(2)}) copy-start(f32[1,512]{1,0:T(1,128)} %param.21) | copy-start | bytes 6148
  280.7 66.8 %all-gather.9.cloned.1.call-start = ((), (), s32[]{:S(2)}) async-start(), calls=%async_computation.3 | async-start | bytes 1966080 | tf_op jit(solution)/shard_map/all_gather | solution.py:101
  321.2 191.5 %all-gather.11.cloned.1.call-start = ((), (), s32[]{:S(2)}) async-start(), calls=%async_computation.4 | async-start | bytes 26738688 | tf_op jit(solution)/shard_map/all_gather | solution.py:103
  347.6 186.6 %collective-permute-start = (bf16[1,512,384]{2,1,0:T(8,128)(2,1)}, bf16[1,512,384]{2,1,0:T(8,128)(2,1)S(1)}, u32[]{:S(2)}, u32[]{:S(2)}) collective-permute-start(bf16[1,512,384]{2,1,0:T(8,128)(2,1)} %bitcast.76), channel_id=1, source_target_pairs={{0,64},{64,0},{1,65},{65,1},{2,66},{66,2},{3,67},{67,3},{4,68},{68... | collective-permute-start | bytes 1179656 | tf_op jit(solution)/shard_map/ppermute | solution.py:27
  512.7 23.7 %copy-start.1 = (bf16[1,2048,384]{2,1,0:T(8,128)(2,1)S(1)}, bf16[1,2048,384]{2,1,0:T(8,128)(2,1)}, u32[]{:S(2)}) copy-start(bf16[1,2048,384]{2,1,0:T(8,128)(2,1)} %param.19) | copy-start | bytes 4718596
  532.5 2.5 collective-permute-start.1
Sparse Core Ops, SparseCore 0:
  14.2 114.7 all-gather.12
  143.7 128.2 all-gather.6
  280.8 38.3 reduce-scatter.1
  321.3 26.1 all-gather.8
  349.5 163.1 all-gather.10
where the time goes:
time: 544 us; the launch traced here: 543 us
  waiting for transfers between devices  431 us (79%)
  blocking collectives  44.3 us (8%)
  matrix products  36.1 us (7%)
  between operations  13.9 us (3%)
  local copies, waits for them, and re-layouts  8.65 us (2%)
  other arithmetic  6.43 us (1%)
    all_gather x1, waiting for transfers between devices, local(): lax.all_gather(features, 'seq', axis=1, tiled=True)  164 us
    all_gather x1, waiting for transfers between devices, local(): lax.all_gather(normed, 'seq', axis=0, tiled=True)  128 us
    all_gather x1, waiting for transfers between devices, entering(): gathered = jax.tree.map(lambda a: lax.all_gather(a, axis), part)  72.5 us
    reduce_scatter x1, waiting for transfers between devices, local(): lax.psum_scatter(partial_sums, 'head', scatter_dimension=0, tiled=True)  38.5 us
    unnamed x1, blocking collectives  35.9 us
    all_gather x1, waiting for transfers between devices, local(): features = lax.all_gather(layer_out, 'head', axis=0, tiled=True)  26.3 us
    dot_general x1, matrix products, local(): jnp.dot(lax.all_gather(features, 'seq', axis=1, tiled=True), encoder, pre...  19.8 us
  transfers between devices with their start and end apart: 7, of which 6 were waited for; matrix products, arithmetic and copies ran while one was open for 5% of the time, Pallas kernels for 0%

commit v1 on v0

--- a/solution.py
+++ b/solution.py
@@ -1,3 +1,4 @@
+import functools
 import jax
 import jax.numpy as jnp
 from jax import lax
@@ -7,6 +8,21 @@
 POOL = 64
 HDIM = 8192
 epsilon = 1e-06
+
+
+def choose_the_turns(a0, bus_axis):
+    return jnp.concatenate(
+        lax.all_to_all(
+            jnp.stack([a0 for _ in range(lax.axis_size(bus_axis))]),
+            axis_name=bus_axis,
+            split_axis=0,
+            concat_axis=0,
+        ),
+        axis=1,
+    )
+
+
+turn_pairs_all_for = functools.partial(choose_the_turns, bus_axis="seq")
 
 
 def entering(part, axis, combine, identity):
@@ -99,11 +115,7 @@
     reduced = lax.psum_scatter(partial_sums, "head", scatter_dimension=0, tiled=True)
     layer_out = (own_rows.astype(jnp.float32) + reduced).astype(jnp.bfloat16)
     features = lax.all_gather(layer_out, "head", axis=0, tiled=True)
-    pre_scores = jnp.dot(
-        lax.all_gather(features, "seq", axis=1, tiled=True),
-        encoder,
-        preferred_element_type=jnp.float32,
-    )
+    pre_scores = jnp.dot(turn_pairs_all_for(features), encoder, preferred_element_type=jnp.float32)
     latent = jax.nn.relu(pre_scores + enc_bias[0])
     pooled = jnp.mean(latent.reshape(-1, POOL, latent_width), axis=1).astype(jnp.bfloat16)
     handoff, monitor = passed_along((layer_out[None], pooled[None]), "section", 1)

time: 544 us -> 772 us (1.42)
  waiting for transfers between devices: 431 us -> 640 us
  local copies, waits for them, and re-layouts: 8.65 us -> 19 us
    all_to_all x0 -> x1, waiting for transfers between devices: none -> 374 us  [choose_the_turns(): lax.all_to_all(jnp.stack([a0 for _ in range(lax.axis_size(bus_axis))]), a...]
    all_gather x1 -> x0, waiting for transfers between devices: 164 us -> none  [local(): lax.all_gather(features, 'seq', axis=1, tiled=True)]
    another operation x0 -> x1, local copies, waits for them, and re-layouts: none -> 8.65 us  [choose_the_turns(): jnp.stack([a0 for _ in range(lax.axis_size(bus_axis))])]
  transfers between devices with their start and end apart: 7 -> 7, of which waited for: 6 -> 6; matrix products, arithmetic and copies ran while one was open for 5% -> 3% of each run, Pallas kernels for 0% -> 0%
where the time goes in v1:
time: 772 us; the launch traced here: 770 us
  waiting for transfers between devices  640 us (83%)
  blocking collectives  44.3 us (6%)
  matrix products  36.1 us (5%)
  local copies, waits for them, and re-layouts  19 us (2%)
  between operations  13.9 us (2%)
  starting transfers between devices  10.2 us (1%)
    all_to_all x1, waiting for transfers between devices, choose_the_turns(): lax.all_to_all(jnp.stack([a0 for _ in range(lax.axis_size(bus_axis))]), a...  374 us
    all_gather x1, waiting for transfers between devices, local(): lax.all_gather(normed, 'seq', axis=0, tiled=True)  128 us
    all_gather x1, waiting for transfers between devices, entering(): gathered = jax.tree.map(lambda a: lax.all_gather(a, axis), part)  72.5 us
    reduce_scatter x1, waiting for transfers between devices, local(): lax.psum_scatter(partial_sums, 'head', scatter_dimension=0, tiled=True)  38.5 us
    unnamed x1, blocking collectives  35.9 us
    all_gather x1, waiting for transfers between devices, local(): features = lax.all_gather(layer_out, 'head', axis=0, tiled=True)  26.4 us
    dot_general x1, matrix products, local(): jnp.dot(turn_pairs_all_for(features), encoder, preferred_element_type=jnp...  19.9 us
  transfers between devices with their start and end apart: 7, of which 6 were waited for; matrix products, arithmetic and copies ran while one was open for 3% of the time, Pallas kernels for 0%

profile of v1, /device:TPU:1, one launch (start us, length us, event | category | flops | bytes accessed | tf_op | source)
XLA Modules:
  0.0 770.2 jit_solution(3780598518025714011)
XLA Ops:
  7.2 1.3 slice.8
  8.6 1.3 broadcast_compare_fusion
  9.9 1.3 copy.32
  11.2 1.3 copy.33
  12.5 1.5 fusion.14
  14.1 1.2 dynamic-slice
  16.8 35.9 %all-reduce = f32[16]{0:T(128)S(1)} all-reduce(f32[16]{0:T(128)S(1)} %slice_dynamic-update-slice_fusion), channel_id=2, replica_groups=mesh['section'=2,'seq'=16,'head'=4] {'seq'}, use_global_device_ids=true, to_apply=%add | all-reduce | flops 16 | bytes 128
  54.3 2.2 convolution_bitcast_fusion
  56.5 72.5 %all-gather.10.cloned.1.call-done = f32[256,128,128]{2,1,0:T(8,128)} async-done(((f32[16,128,128]{2,1,0:T(8,128)}), f32[256,128,128]{2,1,0:T(8,128)}) %all-gather.10.cloned.1.call-update) | async-done | bytes 16777232 | tf_op jit(solution)/shard_map/all_gather | solution.py:30
  129.1 3.6 multiply_reduce_fusion
  132.7 8.4 %psum.7 = f32[128]{0:T(128)S(1)} all-reduce(f32[128]{0:T(128)S(1)} %get-tuple-element.50), channel_id=1, replica_groups=mesh['section'=2,'seq'=16,'head'=4] {'head'}, use_global_device_ids=true, to_apply=%region_3.4 | all-reduce | flops 128 | bytes 1024 | tf_op jit(solution)/shard_map/psum | solution.py:103
  141.1 2.4 fusion.9
  143.6 128.4 %all-gather.6.cloned.1.call-done = bf16[2048,2048]{0,1:T(8,128)(2,1)} async-done(((bf16[128,2048]{0,1:T(8,128)(2,1)}), bf16[2048,2048]{0,1:T(8,128)(2,1)}) %all-gather.6.cloned.1.call-update) | async-done | bytes 8388624 | tf_op jit(solution)/shard_map/all_gather | solution.py:108
  272.0 8.7 %fusion.4 = f32[2048,384]{1,0:T(8,128)} fusion(bf16[2048,2048]{0,1:T(8,128)(2,1)} %all-gather.6.cloned.1.call-done, bf16[1,2048,384]{2,1,0:T(8,128)(2,1)S(1)} %copy-done), kind=kOutput, calls=%fused_computation.6 | convolution fusion | flops 3221225472 | bytes 13107200 | tf_op jit(solution)/shard_map/dot_general | solution.py:107
  280.7 38.5 %reduce-scatter.2.cloned.1.call-done = f32[512,384]{1,0:T(8,128)} async-done(((f32[2048,384]{1,0:T(8,128)}), f32[512,384]{1,0:T(8,128)}) %reduce-scatter.2.cloned.1.call-update) | async-done | bytes 786448 | tf_op jit(solution)/shard_map/reduce_scatter | solution.py:115
  319.2 1.9 fusion.12
  321.2 26.4 %all-gather.8.cloned.1.call-done = bf16[2048,384]{1,0:T(8,128)(2,1)} async-done(((bf16[512,384]{1,0:T(8,128)(2,1)}), bf16[2048,384]{1,0:T(8,128)(2,1)}) %all-gather.8.cloned.1.call-update) | async-done | bytes 1572880 | tf_op jit(solution)/shard_map/all_gather | solution.py:117
  347.5 1.7 copy.30
  349.2 8.7 %stack.2 = bf16[16,2048,384]{1,2,0:T(8,128)(2,1)} broadcast(bf16[2048,384]{0,1:T(8,128)(2,1)S(1)} %copy.30), dimensions={1,2} | broadcast | bytes 26738688 | tf_op jit(solution)/shard_map/stack | solution.py:16
  357.9 6.9 all-to-all-start
  364.8 1.2 collective-permute-start
  366.0 373.7 %all-to-all-done = bf16[16,2048,384]{1,2,0:T(8,128)(2,1)} async-done(((bf16[16,2048,384]{1,2,0:T(8,128)(2,1)}), bf16[16,2048,384]{1,2,0:T(8,128)(2,1)}, u32[]{:S(2)}, u32[]{:S(2)}) %all-to-all-start) | async-done | bytes 25165856 | tf_op jit(solution)/shard_map/all_to_all | solution.py:15
  739.7 19.9 %bitcast_reduce_fusion = f32[32,512]{1,0:T(8,128)S(1)} fusion(bf16[2048,6144]{0,1:T(8,128)(2,1)} %bitcast.19, bf16[1,6144,512]{2,1,0:T(8,128)(2,1)} %param.20, f32[512]{0:T(512)S(1)} %bitcast.83), kind=kOutput, calls=%fused_computation.4 | convolution fusion | flops 12888031232 | bytes 31524864 | tf_op jit(solution)/shard_map/dot_general | solution.py:118
  759.6 1.9 collective-permute-start.1
  (37 shorter events, 5.6 us)
Async XLA Ops:
  7.2 264.8 %copy-start = (bf16[1,2048,384]{2,1,0:T(8,128)(2,1)S(1)}, bf16[1,2048,384]{2,1,0:T(8,128)(2,1)}, u32[]{:S(2)}) copy-start(bf16[1,2048,384]{2,1,0:T(8,128)(2,1)} %param.19) | copy-start | bytes 4718596
  7.2 46.7 %copy-start.5 = (s32[1,128]{1,0:T(1,128)S(1)}, s32[1,128]{1,0:T(1,128)}, u32[]{:S(2)}) copy-start(s32[1,128]{1,0:T(1,128)} %param.16) | copy-start | bytes 1540
  7.2 121.8 %all-gather.10.cloned.1.call-start = ((), (), s32[]{:S(2)}) async-start(), calls=%async_computation.5 | async-start | bytes 17825792 | tf_op jit(solution)/shard_map/all_gather | solution.py:30
  14.0 257.9 %all-gather.6.cloned.1.call-start = ((), (), s32[]{:S(2)}) async-start(), calls=%async_computation.2 | async-start | bytes 8912896 | tf_op jit(solution)/shard_map/all_gather | solution.py:108
  129.1 12.0 %copy-start.4 = (f32[1,2048]{1,0:T(1,128)S(1)}, f32[1,2048]{1,0:T(1,128)}, u32[]{:S(2)}) copy-start(f32[1,2048]{1,0:T(1,128)} %param.17) | copy-start | bytes 24580
  143.5 175.7 %copy-start.3 = (bf16[1,512,384]{2,1,0:T(8,128)(2,1)S(1)}, bf16[1,512,384]{2,1,0:T(8,128)(2,1)}, u32[]{:S(2)}) copy-start(bf16[1,512,384]{2,1,0:T(8,128)(2,1)} %param.18) | copy-start | bytes 1179652
  143.5 175.6 %reduce-scatter.2.cloned.1.call-start = ((), (), s32[]{:S(2)}) async-start(), calls=%async_computation.3 | async-start | bytes 3932160 | tf_op jit(solution)/shard_map/reduce_scatter | solution.py:115
  280.7 66.8 %all-gather.8.cloned.1.call-start = ((), (), s32[]{:S(2)}) async-start(), calls=%async_computation.4 | async-start | bytes 1966080 | tf_op jit(solution)/shard_map/all_gather | solution.py:117
  357.9 6.9 copy-start.2
  357.9 381.8 %copy-start.6 = (f32[1,512]{1,0:T(1,128)S(1)}, f32[1,512]{1,0:T(1,128)}, u32[]{:S(2)}) copy-start(f32[1,512]{1,0:T(1,128)} %param.21) | copy-start | bytes 6148
  357.9 381.8 %all-to-all-start = ((bf16[16,2048,384]{1,2,0:T(8,128)(2,1)}), bf16[16,2048,384]{1,2,0:T(8,128)(2,1)}, u32[]{:S(2)}, u32[]{:S(2)}) async-start(bf16[16,2048,384]{1,2,0:T(8,128)(2,1)} %stack.2), calls=%async_computation.1 | async-start | bytes 50331648 | tf_op jit(solution)/shard_map/all_to_all | solution.py:15
  364.8 396.7 %collective-permute-start = (bf16[1,512,384]{2,1,0:T(8,128)(2,1)S(1)}, bf16[1,512,384]{2,1,0:T(8,128)(2,1)S(1)}, u32[]{:S(2)}, u32[]{:S(2)}) collective-permute-start(bf16[1,512,384]{2,1,0:T(8,128)(2,1)S(1)} %bitcast.79), channel_id=1, source_target_pairs={{0,64},{64,0},{1,65},{65,1},{2,66},{66,2},{3,67},{67,3},{4,68},{68... | collective-permute-start | bytes 1179656 | tf_op jit(solution)/shard_map/ppermute | solution.py:43
  739.7 24.0 %copy-start.1 = (bf16[1,2048,384]{2,1,0:T(8,128)(2,1)S(1)}, bf16[1,2048,384]{2,1,0:T(8,128)(2,1)}, u32[]{:S(2)}) copy-start(bf16[1,2048,384]{2,1,0:T(8,128)(2,1)} %param.19) | copy-start | bytes 4718596
  759.6 2.8 collective-permute-start.1
Sparse Core Ops, SparseCore 0:
  14.2 114.7 all-gather.9
  143.6 128.2 all-gather.5
  280.8 38.3 reduce-scatter.1
  321.3 26.1 all-gather.7
